TPU v7x, 32 devices: a whole 2x2x4 slice. The times are simulated.
32 devices in a mesh: fsdp: 8 (over z, x), tensor: 4 (over y, core).
Axes of the slice: x: 2, y: 2, z: 4, core: 2. Of those that a mesh axis runs over, the one named last changes fastest.
Arguments:
- inputs: float32 [16384, 768], P(('fsdp', 'tensor')), may hold values from -10 to 10
- qkv_weight: bfloat16 [3, 768, 768], P(None, 'fsdp', 'tensor'), may hold values from -0.21875 to 0.21875
- out_weight: bfloat16 [768, 768], P('tensor', 'fsdp'), may hold values from -0.4375 to 0.4375
- conv_weight: float32 [12, 33], replicated, may hold values from -1 to 1
- up_weight: bfloat16 [768, 3072], P('fsdp', 'tensor'), may hold values from -0.21875 to 0.21875
- down_weight: bfloat16 [3072, 768], P('tensor', 'fsdp'), may hold values from -0.109375 to 0.109375
- mix_gain: float32 [768], replicated, may hold values from 0.25 to 1.75
- mix_bias: float32 [768], replicated, may hold values from -1.2 to 1.2
- feed_gain: float32 [768], replicated, may hold values from 0.25 to 1.75
- feed_bias: float32 [768], replicated, may hold values from -1.2 to 1.2
- out_grad: float32 [16384, 768], P(('fsdp', 'tensor')), may hold values from -6 to 6
Outputs:
- output: float32 [16384, 768], P(('fsdp', 'tensor'))
- input_grad: float32 [16384, 768], P(('fsdp', 'tensor'))
- qkv_grad: float32 [3, 768, 768], P(None, 'fsdp', 'tensor')
- out_weight_grad: float32 [768, 768], P('tensor', 'fsdp')
- conv_grad: float32 [12, 33], replicated
- up_grad: float32 [768, 3072], P('fsdp', 'tensor')
- down_grad: float32 [3072, 768], P('tensor', 'fsdp')
- mix_gain_grad: float32 [768], replicated
- mix_bias_grad: float32 [768], replicated
- feed_gain_grad: float32 [768], replicated
- feed_bias_grad: float32 [768], replicated
All inputs are finite; a program needn't handle non-finite values.
Results may differ from a plain program's by a relative error of at most 0.014.
Values may be sent and summed in bfloat16 or wider, within the bound.
No kernel may reach another device: no remote copies, remote signals or barrier semaphores. Data moves between devices by JAX's collectives and lax.ppermute only.
A program may use at most 192 MiB of HBM per device.

v0:
```python
import jax
import jax.numpy as jnp
from jax import lax
from jax.sharding import PartitionSpec as P

HD = 64
LANDMARKS = 64
ITERS = 6


def in_blocks(value, dim, count):
    lengths = value.shape
    tiles = value.reshape(*lengths[:dim], count, lengths[dim] // count, *lengths[dim + 1 :])
    return jnp.moveaxis(tiles, dim, 0)


def sum_at_owner(value, axis, dim):
    tiles = in_blocks(value, dim, lax.axis_size(axis))
    arrived = lax.all_to_all(tiles, axis, split_axis=0, concat_axis=0, tiled=True)
    return arrived.astype(jnp.float32).sum(axis=0)


def landmarks(query, key):
    heads, length, width = query.shape
    factor = width ** (-0.25)
    scaled_q = query * factor
    scaled_k = key * factor
    marks_q = jnp.mean(scaled_q.reshape(heads, LANDMARKS, length // LANDMARKS, width), axis=2)
    marks_k = jnp.mean(scaled_k.reshape(heads, LANDMARKS, length // LANDMARKS, width), axis=2)
    inner = jnp.einsum("hid,hjd->hij", marks_q, marks_k, precision=lax.Precision.HIGHEST)
    kernel_two = jax.nn.softmax(inner, axis=-1)
    return (scaled_q, scaled_k, marks_q, marks_k, kernel_two)


def column_peak(query, key):
    kernel_two = landmarks(query, key)[4]
    return jnp.max(jnp.sum(kernel_two, axis=1), axis=1)


def mixing(query, key, value, conv, inverse):
    high = lax.Precision.HIGHEST
    scaled_q, scaled_k, marks_q, marks_k, kernel_two = landmarks(query, key)
    length = query.shape[1]
    kernel_one = jax.nn.softmax(
        jnp.einsum("hnd,hjd->hnj", scaled_q, marks_k, precision=high), axis=-1
    )
    kernel_three = jax.nn.softmax(
        jnp.einsum("hid,hnd->hin", marks_q, scaled_k, precision=high), axis=-1
    )
    approx = jnp.swapaxes(kernel_two, 1, 2) * inverse[:, None, None]
    ident = jnp.eye(kernel_two.shape[1], dtype=jnp.float32)
    for step in range(ITERS):
        prod = jnp.einsum("hij,hjk->hik", kernel_two, approx, precision=high)
        inner = 7.0 * ident - prod
        inner = 15.0 * ident - jnp.einsum("hij,hjk->hik", prod, inner, precision=high)
        inner = 13.0 * ident - jnp.einsum("hij,hjk->hik", prod, inner, precision=high)
        approx = jnp.einsum("hij,hjk->hik", 0.25 * approx, inner, precision=high)
    summary = jnp.einsum("hin,hnd->hid", kernel_three, value, precision=high)
    carried = jnp.einsum("hij,hjd->hid", approx, summary, precision=high)
    mixed = jnp.einsum("hnj,hjd->hnd", kernel_one, carried, precision=high)
    margin = conv.shape[1] // 2
    padded = jnp.pad(value, ((0, 0), (margin, margin), (0, 0)))
    for tap in range(conv.shape[1]):
        mixed = mixed + conv[:, tap][:, None, None] * padded[:, tap : tap + length, :]
    return mixed


def gelu_tanh(value):
    return jax.nn.gelu(value, approximate=True)


def norm_forward(rows, gain, shift):
    center = rows - jnp.mean(rows, axis=-1, keepdims=True)
    spread = jnp.mean(center * center, axis=-1, keepdims=True)
    factor = lax.rsqrt(spread + 1e-05)
    normed = center * factor
    return (normed * gain + shift, normed, factor)


def norm_backward(cotan, normed, factor, gain):
    scaled = cotan * gain
    return factor * (
        scaled
        - jnp.mean(scaled, axis=-1, keepdims=True)
        - normed * jnp.mean(scaled * normed, axis=-1, keepdims=True)
    )


def norm_params(cotan, normed):
    return (jnp.sum(cotan * normed, axis=0), jnp.sum(cotan, axis=0))


def shards(
    inputs,
    qkv_weight,
    out_weight,
    conv_weight,
    up_weight,
    down_weight,
    mix_gain,
    mix_bias,
    feed_gain,
    feed_bias,
    out_grad,
):
    place = lax.axis_index("tensor")
    gathered_in = lax.all_gather(inputs.astype(jnp.bfloat16), "tensor", axis=0, tiled=True)
    length = gathered_in.shape[0]
    w_qkv, w_out, w_up, w_down = (
        lax.all_gather(qkv_weight, "fsdp", axis=1, tiled=True),
        lax.all_gather(out_weight, "fsdp", axis=1, tiled=True),
        lax.all_gather(up_weight, "fsdp", axis=0, tiled=True),
        lax.all_gather(down_weight, "fsdp", axis=1, tiled=True),
    )
    columns = w_qkv.shape[2]
    local_heads = columns // HD
    qkv = jnp.einsum("nd,kdc->knc", gathered_in, w_qkv, preferred_element_type=jnp.float32)

    def split_heads(block):
        return block.reshape(length, local_heads, HD).transpose(1, 0, 2)

    query, key, value = (split_heads(qkv[0]), split_heads(qkv[1]), split_heads(qkv[2]))
    conv_local = lax.dynamic_slice_in_dim(conv_weight, place * local_heads, local_heads, 0)
    peak_local = column_peak(query, key)
    peak = lax.pmax(peak_local, "fsdp")
    inverse = 1.0 / peak
    mixed, mixing_back = jax.vjp(mixing, query, key, value, conv_local, inverse)
    context = mixed.transpose(1, 0, 2).reshape(length, columns).astype(jnp.bfloat16)
    attended = lax.psum_scatter(
        jnp.dot(context, w_out, preferred_element_type=jnp.float32),
        "tensor",
        scatter_dimension=0,
        tiled=True,
    )
    mixed_rows, normed_mix, factor_mix = norm_forward(inputs + attended, mix_gain, mix_bias)
    mixed_low = lax.all_gather(mixed_rows.astype(jnp.bfloat16), "tensor", axis=0, tiled=True)
    up_rows = jnp.dot(mixed_low, w_up, preferred_element_type=jnp.float32)
    act, gelu_back = jax.vjp(gelu_tanh, up_rows)
    act_low = act.astype(jnp.bfloat16)
    fed = lax.psum_scatter(
        jnp.dot(act_low, w_down, preferred_element_type=jnp.float32).astype(jnp.bfloat16),
        "tensor",
        scatter_dimension=0,
        tiled=True,
    ).astype(jnp.float32)
    output, normed_feed, factor_feed = norm_forward(mixed_rows + fed, feed_gain, feed_bias)
    grad_feed = norm_backward(out_grad, normed_feed, factor_feed, feed_gain)
    feed_gain_part, feed_bias_part = norm_params(out_grad, normed_feed)
    grad_down = lax.all_gather(grad_feed.astype(jnp.bfloat16), "tensor", axis=0, tiled=True)
    down_grad = jnp.einsum("nf,nd->fd", act_low, grad_down, preferred_element_type=jnp.float32)
    grad_act = jnp.einsum("nd,fd->nf", grad_down, w_down, preferred_element_type=jnp.float32)
    grad_up = gelu_back(grad_act)[0].astype(jnp.bfloat16)
    up_grad = jnp.einsum("nd,nf->df", mixed_low, grad_up, preferred_element_type=jnp.float32)
    grad_mixed_rows = grad_feed + lax.psum_scatter(
        jnp.einsum("nf,df->nd", grad_up, w_up, preferred_element_type=jnp.float32).astype(
            jnp.bfloat16
        ),
        "tensor",
        scatter_dimension=0,
        tiled=True,
    ).astype(jnp.float32)
    grad_mix = norm_backward(grad_mixed_rows, normed_mix, factor_mix, mix_gain)
    mix_gain_part, mix_bias_part = norm_params(grad_mixed_rows, normed_mix)
    grad_attended = lax.all_gather(grad_mix.astype(jnp.bfloat16), "tensor", axis=0, tiled=True)
    out_weight_grad = jnp.einsum(
        "nc,nd->cd", context, grad_attended, preferred_element_type=jnp.float32
    )
    grad_context = jnp.einsum("nd,cd->nc", grad_attended, w_out, preferred_element_type=jnp.float32)
    grad_mixed = grad_context.reshape(length, local_heads, HD).transpose(1, 0, 2)
    grad_query, grad_key, grad_value, grad_conv, grad_inverse = mixing_back(grad_mixed)
    grad_peak = -grad_inverse * inverse * inverse
    head_total = conv_weight.shape[0]
    peak_full = lax.dynamic_update_slice_in_dim(
        jnp.zeros((head_total,), jnp.float32), grad_peak, place * local_heads, 0
    )
    conv_full = lax.dynamic_update_slice_in_dim(
        jnp.zeros(conv_weight.shape, jnp.float32), grad_conv, place * local_heads, 0
    )
    norm_stack = jnp.stack([mix_gain_part, mix_bias_part, feed_gain_part, feed_bias_part])
    peak_sum, conv_grad, norm_sum = lax.psum((peak_full, conv_full, norm_stack), ("fsdp", "tensor"))
    peak_total = lax.dynamic_slice_in_dim(peak_sum, place * local_heads, local_heads, 0)
    owner = jnp.where(peak_local == peak, peak_total, 0.0)
    unused, peak_back = jax.vjp(column_peak, query, key)
    extra_query, extra_key = peak_back(owner)

    def merge_heads(block):
        return block.transpose(1, 0, 2).reshape(length, columns)

    grad_qkv = jnp.stack(
        [
            merge_heads(grad_query + extra_query),
            merge_heads(grad_key + extra_key),
            merge_heads(grad_value),
        ]
    ).astype(jnp.bfloat16)
    qkv_grad = jnp.einsum("nd,knc->kdc", gathered_in, grad_qkv, preferred_element_type=jnp.float32)
    input_grad = grad_mix + lax.psum_scatter(
        jnp.einsum("knc,kdc->nd", grad_qkv, w_qkv, preferred_element_type=jnp.float32).astype(
            jnp.bfloat16
        ),
        "tensor",
        scatter_dimension=0,
        tiled=True,
    ).astype(jnp.float32)
    qkv_share, out_share, up_share, down_share = (
        sum_at_owner(qkv_grad.astype(jnp.bfloat16), "fsdp", 1),
        sum_at_owner(out_weight_grad.astype(jnp.bfloat16), "fsdp", 1),
        sum_at_owner(up_grad.astype(jnp.bfloat16), "fsdp", 0),
        sum_at_owner(down_grad.astype(jnp.bfloat16), "fsdp", 1),
    )
    return (
        output,
        input_grad,
        qkv_share,
        out_share,
        conv_grad,
        up_share,
        down_share,
        norm_sum[0],
        norm_sum[1],
        norm_sum[2],
        norm_sum[3],
    )


def solution(mesh):
    placed = (
        P(("fsdp", "tensor"), None),
        P(None, "fsdp", "tensor"),
        P("tensor", "fsdp"),
        P(),
        P("fsdp", "tensor"),
        P("tensor", "fsdp"),
        P(),
        P(),
        P(),
        P(),
        P(("fsdp", "tensor"), None),
    )
    return jax.shard_map(
        shards,
        mesh=mesh,
        in_specs=placed,
        out_specs=(
            P(("fsdp", "tensor"), None),
            P(("fsdp", "tensor"), None),
            P(None, "fsdp", "tensor"),
            P("tensor", "fsdp"),
            P(),
            P("fsdp", "tensor"),
            P("tensor", "fsdp"),
            P(),
            P(),
            P(),
            P(),
        ),
        check_vma=False,
    )
```

profile of v0, /device:TPU:0, one launch (start us, length us, event | category | flops | bytes accessed | tf_op | source)
XLA Modules:
  0.0 735.5 jit_solution(5595995136005372708)
XLA Ops:
  12.9 35.1 %all_gather.26 = bf16[192,768]{0,1:T(8,128)(2,1)} all-gather(bf16[192,96]{0,1:T(8,128)(2,1)S(1)} %copy.111), channel_id=1, replica_groups=mesh['fsdp'=8,'tensor'=4] {'fsdp'}, dimensions={1}, use_global_device_ids=true | all-gather | bytes 331776 | tf_op jit(solution)/shard_map/all_gather | solution.py:111
  48.0 38.3 %all_gather.24 = bf16[3,768,192]{2,0,1:T(4,128)(2,1)S(1)} all-gather(bf16[3,96,192]{2,0,1:T(4,128)(2,1)S(1)} %copy.100), channel_id=1, replica_groups=mesh['fsdp'=8,'tensor'=4] {'fsdp'}, dimensions={1}, use_global_device_ids=true | all-gather | bytes 995328 | tf_op jit(solution)/shard_map/all_gather | solution.py:110
  87.5 4.6 convolution_bitcast_fusion
  99.6 4.4 bitcast_reduce_fusion
  110.2 19.7 %pmax.7 = f32[3]{0:T(128)S(1)} all-reduce(f32[3]{0:T(128)S(1)} %reduce_max.37), channel_id=1, replica_groups=mesh['fsdp'=8,'tensor'=4] {'fsdp'}, use_global_device_ids=true, to_apply=%region_8.0 | all-reduce | flops 3 | bytes 24 | tf_op jit(solution)/shard_map/pmax | solution.py:125
  145.2 14.7 %fusion.56 = bf16[3,2048,64]{1,2,0:T(8,128)(2,1)S(1)} fusion(f32[3,64,64]{2,1,0:T(8,128)S(1)} %fusion.210, f32[3,2048,64]{1,2,0:T(8,128)S(1)} %bitcast.257, f32[3]{0:T(128)S(1)} %copy-done.126, f32[3]{0:T(128)S(1)} %copy-done.138, f32[3]{0:T(128)S(1)} %copy-done.139, f32[3]{0:T(128)S(1)} %copy-done.140, f32[3]{0:T(128)S(1)} %copy-done.141, ...), kind=kOutput, calls=%fused_computation.69 | convolution fusion | flops 328728576 | bytes 4006284 | tf_op jit(solution)/shard_map/jvp(hnj,hjd->hnd)/dot_general | solution.py:60
  165.2 55.7 %reduce-scatter.5.cloned.1.call-done = f32[512,768]{1,0:T(8,128)} async-done(((f32[2048,768]{1,0:T(8,128)}), f32[512,768]{1,0:T(8,128)}) %reduce-scatter.5.cloned.1.call-update) | async-done | bytes 1572880 | tf_op jit(solution)/shard_map/reduce_scatter | solution.py:129
  225.6 27.8 %all-gather.9.cloned.1.call-done = bf16[2048,768]{1,0:T(8,128)(2,1)} async-done(((bf16[512,768]{1,0:T(8,128)(2,1)}), bf16[2048,768]{1,0:T(8,128)(2,1)}) %all-gather.9.cloned.1.call-update) | async-done | bytes 3145744 | tf_op jit(solution)/shard_map/all_gather | solution.py:136
  253.4 7.5 %fusion.212 = f32[2048,768]{1,0:T(8,128)} fusion(bf16[2048,768]{1,0:T(8,128)(2,1)} %all-gather.9.cloned.1.call-done, bf16[768,768]{1,0:T(8,128)(2,1)} %all-gather.11.cloned.1.call-done), kind=kOutput, calls=%fused_computation.447 | convolution fusion | flops 2415919104 | bytes 10616832 | tf_op jit(solution)/shard_map/dot_general | solution.py:137
  260.9 36.0 %all-gather.13.cloned.1.call-done = bf16[768,768]{0,1:T(8,128)(2,1)} async-done(((bf16[768,96]{0,1:T(8,128)(2,1)}), bf16[768,768]{0,1:T(8,128)(2,1)}) %all-gather.13.cloned.1.call-update) | async-done | bytes 1179664 | tf_op jit(solution)/shard_map/all_gather | solution.py:113
  296.9 8.6 %convolution_convert_fusion.1 = bf16[2048,768]{1,0:T(8,128)(2,1)} fusion(bf16[768,768]{0,1:T(8,128)(2,1)} %all-gather.13.cloned.1.call-done, f32[2048,768]{1,0:T(8,128)} %fusion.212), kind=kOutput, calls=%fused_computation.15 | convolution fusion | flops 2431647744 | bytes 10616832 | tf_op jit(solution)/shard_map/dot_general | solution.py:141
  305.6 36.1 %reduce-scatter.7.cloned.1.call-done = bf16[512,768]{1,0:T(8,128)(2,1)} async-done(((bf16[2048,768]{1,0:T(8,128)(2,1)}), bf16[512,768]{1,0:T(8,128)(2,1)}) %reduce-scatter.7.cloned.1.call-update) | async-done | bytes 786448 | tf_op jit(solution)/shard_map/reduce_scatter | solution.py:140
  348.3 28.4 %all-gather.15.cloned.1.call-done = bf16[2048,768]{1,0:T(8,128)(2,1)} async-done(((bf16[512,768]{1,0:T(8,128)(2,1)}), bf16[2048,768]{1,0:T(8,128)(2,1)}) %all-gather.15.cloned.1.call-update) | async-done | bytes 3145744 | tf_op jit(solution)/shard_map/all_gather | solution.py:149
  376.7 8.5 %fusion.9 = bf16[2048,768]{1,0:T(8,128)(2,1)S(1)} fusion(f32[2048,768]{1,0:T(8,128)} %fusion.212, bf16[2048,768]{1,0:T(8,128)(2,1)} %all-gather.15.cloned.1.call-done, bf16[768,768]{0,1:T(8,128)(2,1)} %all-gather.13.cloned.1.call-done), kind=kOutput, calls=%fused_computation.11 | convolution fusion | flops 2447376384 | bytes 13762560 | tf_op jit(solution)/shard_map/nd,fd->nf/dot_general | solution.py:151
  391.0 38.0 %reduce-scatter.9.cloned.1.call-done = bf16[512,768]{1,0:T(8,128)(2,1)} async-done(((bf16[2048,768]{1,0:T(8,128)(2,1)}), bf16[512,768]{1,0:T(8,128)(2,1)}) %reduce-scatter.9.cloned.1.call-update) | async-done | bytes 786448 | tf_op jit(solution)/shard_map/reduce_scatter | solution.py:154
  436.8 8.0 %convolution_convert_fusion.2 = bf16[768,768]{0,1:T(8,128)(2,1)} fusion(bf16[2048,768]{1,0:T(8,128)(2,1)} %all-gather.15.cloned.1.call-done, f32[2048,768]{1,0:T(8,128)} %fusion.212), kind=kOutput, calls=%fused_computation.133 | convolution fusion | flops 2430664704 | bytes 10616832 | tf_op jit(solution)/shard_map/nf,nd->fd/dot_general | solution.py:150
  444.7 5.5 all-to-all-start.3
  450.4 12.3 %all-gather.17.cloned.1.call-done = bf16[2048,768]{1,0:T(8,128)(2,1)} async-done(((bf16[512,768]{1,0:T(8,128)(2,1)}), bf16[2048,768]{1,0:T(8,128)(2,1)}) %all-gather.17.cloned.1.call-update) | async-done | bytes 3145744 | tf_op jit(solution)/shard_map/all_gather | solution.py:164
  465.8 8.2 %multiply_reduce_fusion.34 = (f32[3]{0:T(128)S(1)}, f32[3]{0:T(128)S(1)}, f32[3]{0:T(128)S(1)}, f32[3]{0:T(128)S(1)}, f32[3]{0:T(128)S(1)}, /*index=5*/f32[3]{0:...) fusion(f32[3,2048,64]{1,2,0:T(8,128)S(1)} %bitcast.250, ...), kind=kLoop, calls=%fused_computation.117 | loop fusion | flops 14155722 | bytes 3145944 | tf_op jit(solution)/shard_map/transpose(jvp())/reduce_sum | solution.py:64
  489.6 7.8 %multiply_reduce_fusion.33 = (f32[3]{0:T(128)S(1)}, f32[3]{0:T(128)S(1)}, f32[3]{0:T(128)S(1)}, f32[3]{0:T(128)S(1)}, f32[3]{0:T(128)S(1)}, /*index=5*/f32[3]{0:...) fusion(f32[3,2048,64]{1,2,0:T(8,128)S(1)} %bitcast.252, ...), kind=kLoop, calls=%fused_computation.116 | loop fusion | flops 12976083 | bytes 7864536 | tf_op jit(solution)/shard_map/transpose(jvp())/reduce_sum | solution.py:64
  504.5 40.0 %all-reduce.67 = (f32[12]{0:T(128)S(1)}, f32[12,33]{1,0:T(8,128)}, f32[4,768]{1,0:T(4,128)}) all-reduce(f32[12]{0:T(128)S(1)} %fusion.168, f32[12,33]{1,0:T(8,128)S(1)} %dynamic_update_slice.7, f32[4,768]{1,0:T(4,128)S(1)} %pad_maximum_fusion.3), channel_id=1, replica_groups=mesh['fsdp'=8,'tensor'=4] {'fsdp','tensor'}, use_global_device_ids=true, to_apply=%region_26.27 | all-reduce | flops 3480 | bytes 27840 | tf_op jit(solution)/shard_map/psum | solution.py:180
  549.8 7.4 %broadcast_multiply_fusion.1 = (f32[3,2048,64]{1,2,0:T(8,128)}, f32[3,2048,64]{1,2,0:T(8,128)}, f32[3,2048,64]{1,2,0:T(8,128)}, f32[3,2048,64]{1,2,0:T(8,128)}, ...) fusion(f32[3,2048,64]{1,2,0:T(8,128)S(1)} %bitcast.253, ...), kind=kLoop, calls=%fused_computation.216 | loop fusion | flops 4718592 | bytes 20447376 | tf_op jit(solution)/shard_map/transpose(jvp())/mul | solution.py:64
  557.4 11.1 %broadcast_multiply_fusion = (f32[3,2048,64]{1,2,0:T(8,128)}, f32[3,2048,64]{1,2,0:T(8,128)}, f32[3,2048,64]{1,2,0:T(8,128)}, f32[3,2048,64]{1,2,0:T(8,128)}, f3...) fusion(f32[3,2048,64]{1,2,0:T(8,128)S(1)} %bitcast.254, ...), kind=kLoop, calls=%fused_computation.215 | loop fusion | flops 7077888 | bytes 29884632 | tf_op jit(solution)/shard_map/transpose(jvp())/mul | solution.py:64
  597.2 5.2 fusion.54
  605.5 18.7 %pad_add_fusion = f32[3,2080,64]{1,2,0:T(8,128)S(1)} fusion(f32[3,2048,64]{1,2,0:T(8,128)S(1)} %copy-done.10, f32[3,2048,64]{1,2,0:T(8,128)S(1)} %copy-done.11, f32[3,2048,64]{1,2,0:T(8,128)S(1)} %copy-done.12, f32[3,2048,64]{1,2,0:T(8,128)} %get-tuple-element.129, f32[3,2048,64]{1,2,0:T(8,128)} %get-tuple-element.130, ...), kind=kLoop, calls=%fused_computation.74 | loop fusion | flops 10383360 | bytes 44064768 | tf_op jit(solution)/shard_map/transpose(jvp())/add_any | solution.py:64
  624.2 7.5 %fusion.53 = bf16[3,2048,64]{1,2,0:T(8,128)(2,1)S(1)} fusion(f32[3,64,64]{2,1,0:T(8,128)S(1)} %copy-done.52, f32[3,2048,64]{1,2,0:T(8,128)} %get-tuple-element.119, f32[3,2048,64]{1,2,0:T(8,128)} %get-tuple-element.120, f32[3,2048,64]{1,2,0:T(8,128)} %get-tuple-element.121, f32[3,2048,64]{1,2,0:T(8,128)} %get-tuple-element.123, ...), kind=kOutput, calls=%fused_computation.66 | convolution fusion | flops 305528832 | bytes 13419264 | tf_op jit(solution)/shard_map/transpose(jvp(hin,hnd->hid))/dot_general | solution.py:58
  632.6 4.2 bitcast_convert_fusion
  636.8 6.5 convolution_convert_fusion.3
  643.3 5.4 all-to-all-start.2
  652.7 24.3 %all-to-all-done.2 = bf16[8,96,768]{2,1,0:T(8,128)(2,1)S(1)} async-done(((bf16[8,96,768]{2,1,0:T(8,128)(2,1)}), bf16[8,96,768]{2,1,0:T(8,128)(2,1)S(1)}, u32[]{:S(2)}, u32[]{:S(2)}) %all-to-all-start.2) | async-done | bytes 1179680 | tf_op jit(solution)/shard_map/all_to_all | solution.py:19
  680.5 5.0 fusion.61
  700.4 24.3 %all-to-all-done = bf16[8,3,96,192]{2,3,1,0:T(8,128)(2,1)S(1)} async-done(((bf16[8,3,96,192]{2,3,1,0:T(8,128)(2,1)}), bf16[8,3,96,192]{2,3,1,0:T(8,128)(2,1)S(1)}, u32[]{:S(2)}, u32[]{:S(2)}) %all-to-all-start) | async-done | bytes 884768 | tf_op jit(solution)/shard_map/all_to_all | solution.py:19
  (522 shorter events, 152.2 us)
Async XLA Ops:
  8.0 78.3 %all-gather.7.cloned.1.call-start = ((), (), s32[]{:S(2)}) async-start(), calls=%async_computation.8 | async-start | bytes 3932160 | tf_op jit(solution)/shard_map/all_gather | solution.py:107
  10.5 210.4 %reduce-scatter.5.cloned.1.call-start = ((), (), s32[]{:S(2)}) async-start(), calls=%async_computation.9 | async-start | bytes 7864320 | tf_op jit(solution)/shard_map/reduce_scatter | solution.py:129
  11.8 133.1 %copy-start.102 = (f32[3]{0:T(128)}, f32[3]{0:T(128)S(1)}, u32[]{:S(2)}) copy-start(f32[3]{0:T(128)S(1)} %get-tuple-element.89) | copy-start | bytes 40
  11.8 133.1 %copy-start.104 = (f32[3]{0:T(128)}, f32[3]{0:T(128)S(1)}, u32[]{:S(2)}) copy-start(f32[3]{0:T(128)S(1)} %get-tuple-element.90) | copy-start | bytes 40
  93.9 10.0 %copy-start.2 = (f32[1,2048,192]{1,2,0:T(8,128)}, f32[1,2048,192]{1,2,0:T(8,128)S(1)}, u32[]{:S(2)}) copy-start(f32[1,2048,192]{1,2,0:T(8,128)S(1)} %get-tuple-element.116) | copy-start | bytes 4718596
  139.9 296.2 %copy-start.91 = (f32[3,64]{1,0:T(4,128)}, f32[3,64]{1,0:T(4,128)S(1)}, u32[]{:S(2)}) copy-start(f32[3,64]{1,0:T(4,128)S(1)} %get-tuple-element.154) | copy-start | bytes 2308
  144.5 15.4 %copy-start.85 = (f32[3,64,64]{2,1,0:T(8,128)}, f32[3,64,64]{2,1,0:T(8,128)S(1)}, u32[]{:S(2)}) copy-start(f32[3,64,64]{2,1,0:T(8,128)S(1)} %fusion.210) | copy-start | bytes 147460
  145.2 15.6 %copy-start.22 = (bf16[192,768]{0,1:T(8,128)(2,1)S(1)}, bf16[192,768]{0,1:T(8,128)(2,1)}, u32[]{:S(2)}) copy-start(bf16[192,768]{0,1:T(8,128)(2,1)} %all_gather.26) | copy-start | bytes 884740
  164.6 61.0 %all-gather.11.cloned.1.call-start = ((), (), s32[]{:S(2)}) async-start(), calls=%async_computation.11 | async-start | bytes 1327104 | tf_op jit(solution)/shard_map/all_gather | solution.py:112
  165.1 88.3 %all-gather.9.cloned.1.call-start = ((), (), s32[]{:S(2)}) async-start(), calls=%async_computation.10 | async-start | bytes 3932160 | tf_op jit(solution)/shard_map/all_gather | solution.py:136
  224.9 72.0 %all-gather.13.cloned.1.call-start = ((), (), s32[]{:S(2)}) async-start(), calls=%async_computation.12 | async-start | bytes 1327104 | tf_op jit(solution)/shard_map/all_gather | solution.py:113
  225.5 116.2 %reduce-scatter.7.cloned.1.call-start = ((), (), s32[]{:S(2)}) async-start(), calls=%async_computation.13 | async-start | bytes 3932160 | tf_op jit(solution)/shard_map/reduce_scatter | solution.py:140
  305.5 71.2 %all-gather.15.cloned.1.call-start = ((), (), s32[]{:S(2)}) async-start(), calls=%async_computation.14 | async-start | bytes 3932160 | tf_op jit(solution)/shard_map/all_gather | solution.py:149
  348.2 80.8 %reduce-scatter.9.cloned.1.call-start = ((), (), s32[]{:S(2)}) async-start(), calls=%async_computation.15 | async-start | bytes 3932160 | tf_op jit(solution)/shard_map/reduce_scatter | solution.py:154
  376.7 10.2 %copy-start.157 = (bf16[768,768]{1,0:T(8,128)(2,1)S(1)}, bf16[768,768]{1,0:T(8,128)(2,1)}, u32[]{:S(2)}) copy-start(bf16[768,768]{1,0:T(8,128)(2,1)} %all-gather.11.cloned.1.call-done) | copy-start | bytes 3538948
  390.9 71.8 %all-gather.17.cloned.1.call-start = ((), (), s32[]{:S(2)}) async-start(), calls=%async_computation.16 | async-start | bytes 3932160 | tf_op jit(solution)/shard_map/all_gather | solution.py:164
  444.7 198.6 %all-to-all-start.3 = ((bf16[8,768,96]{1,2,0:T(8,128)(2,1)}), bf16[8,768,96]{1,2,0:T(8,128)(2,1)}, u32[]{:S(2)}, u32[]{:S(2)}) async-start(bf16[8,768,96]{1,2,0:T(8,128)(2,1)} %bitcast.70), calls=%async_computation.7 | async-start | bytes 2359296 | tf_op jit(solution)/shard_map/all_to_all | solution.py:19
  450.3 275.5 %reduce-scatter.11.cloned.1.call-start = ((), (), s32[]{:S(2)}) async-start(), calls=%async_computation.17 | async-start | bytes 3932160 | tf_op jit(solution)/shard_map/reduce_scatter | solution.py:197
  498.3 49.1 %copy-start.35 = (f32[3,64,64]{2,1,0:T(8,128)S(1)}, f32[3,64,64]{2,1,0:T(8,128)}, u32[]{:S(2)}) copy-start(f32[3,64,64]{2,1,0:T(8,128)} %copy-done.34) | copy-start | bytes 147460
  504.5 65.8 %copy-start.51 = (f32[3,64,64]{2,1,0:T(8,128)}, f32[3,64,64]{2,1,0:T(8,128)S(1)}, u32[]{:S(2)}) copy-start(f32[3,64,64]{2,1,0:T(8,128)S(1)} %fusion.214) | copy-start | bytes 147460
  557.4 11.2 %copy-start.16 = (f32[3,2048,64]{1,2,0:T(8,128)S(1)}, f32[3,2048,64]{1,2,0:T(8,128)}, u32[]{:S(2)}) copy-start(f32[3,2048,64]{1,2,0:T(8,128)} %copy-done.14) | copy-start | bytes 4718596
  557.4 11.2 %copy-start.86 = (f32[3,64,64]{2,1,0:T(8,128)S(1)}, f32[3,64,64]{2,1,0:T(8,128)}, u32[]{:S(2)}) copy-start(f32[3,64,64]{2,1,0:T(8,128)} %copy-done.85) | copy-start | bytes 147460
  605.5 18.7 %copy-start.52 = (f32[3,64,64]{2,1,0:T(8,128)S(1)}, f32[3,64,64]{2,1,0:T(8,128)}, u32[]{:S(2)}) copy-start(f32[3,64,64]{2,1,0:T(8,128)} %copy-done.51) | copy-start | bytes 147460
  624.2 8.4 %copy-start.33 = (bf16[3,768,192]{2,0,1:T(4,128)(2,1)S(1)}, bf16[3,768,192]{2,0,1:T(4,128)(2,1)}, u32[]{:S(2)}) copy-start(bf16[3,768,192]{2,0,1:T(4,128)(2,1)} %copy-done.32) | copy-start | bytes 2654212
  624.2 8.4 %copy-start.158 = (bf16[3,2048,64]{1,2,0:T(8,128)(2,1)S(1)}, bf16[3,2048,64]{1,2,0:T(8,128)(2,1)}, u32[]{:S(2)}) copy-start(bf16[3,2048,64]{1,2,0:T(8,128)(2,1)} %fusion.54) | copy-start | bytes 2359300
  624.2 8.4 %copy-start.160 = (bf16[3,2048,64]{1,2,0:T(8,128)(2,1)S(1)}, bf16[3,2048,64]{1,2,0:T(8,128)(2,1)}, u32[]{:S(2)}) copy-start(bf16[3,2048,64]{1,2,0:T(8,128)(2,1)} %fusion.55) | copy-start | bytes 2359300
  643.3 33.7 %all-to-all-start.2 = ((bf16[8,96,768]{2,1,0:T(8,128)(2,1)}), bf16[8,96,768]{2,1,0:T(8,128)(2,1)S(1)}, u32[]{:S(2)}, u32[]{:S(2)}) async-start(bf16[8,96,768]{2,1,0:T(8,128)(2,1)} %bitcast.273), calls=%async_computation.6 | async-start | bytes 2359296 | tf_op jit(solution)/shard_map/all_to_all | solution.py:19
  651.4 29.1 %copy-start.79 = (bf16[3,2048,64]{1,2,0:T(8,128)(2,1)S(1)}, bf16[3,2048,64]{1,2,0:T(8,128)(2,1)}, u32[]{:S(2)}) copy-start(bf16[3,2048,64]{1,2,0:T(8,128)(2,1)} %copy-done.78) | copy-start | bytes 2359300
  651.8 28.7 %copy-start.159 = (bf16[3,2048,64]{1,2,0:T(8,128)(2,1)S(1)}, bf16[3,2048,64]{1,2,0:T(8,128)(2,1)}, u32[]{:S(2)}) copy-start(bf16[3,2048,64]{1,2,0:T(8,128)(2,1)} %fusion.54) | copy-start | bytes 2359300
  677.0 15.4 %all-to-all-start.1 = ((bf16[8,192,96]{2,1,0:T(8,128)(2,1)}), bf16[8,192,96]{2,1,0:T(8,128)(2,1)S(1)}, u32[]{:S(2)}, u32[]{:S(2)}) async-start(bf16[8,192,96]{2,1,0:T(8,128)(2,1)} %bitcast.249), calls=%async_computation.5 | async-start | bytes 786432 | tf_op jit(solution)/shard_map/all_to_all | solution.py:19
  692.4 32.3 %all-to-all-start = ((bf16[8,3,96,192]{2,3,1,0:T(8,128)(2,1)}), bf16[8,3,96,192]{2,3,1,0:T(8,128)(2,1)S(1)}, u32[]{:S(2)}, u32[]{:S(2)}) async-start(bf16[8,3,96,192]{2,3,1,0:T(8,128)(2,1)} %bitcast.248), calls=%async_computation.4 | async-start | bytes 2359296 | tf_op jit(solution)/shard_map/all_to_all | solution.py:19
  699.0 26.8 %copy-start.19 = (f32[512,768]{1,0:T(8,128)S(1)}, f32[512,768]{1,0:T(8,128)}, u32[]{:S(2)}) copy-start(f32[512,768]{1,0:T(8,128)} %get-tuple-element.108) | copy-start | bytes 4718596
  (146 other events, 463.8 us)
Sparse Core Ops, SparseCore 0:
  11.0 31.2 all-gather.6
  164.7 56.1 reduce-scatter.4
  391.0 37.8 reduce-scatter.8
  636.9 38.9 reduce-scatter.10
Sparse Core Ops, SparseCore 1:
  167.2 38.7 all-gather.10
  225.0 28.3 all-gather.8
  255.5 41.4 all-gather.12
  305.6 36.1 reduce-scatter.6
  348.3 28.3 all-gather.14
  434.3 28.3 all-gather.16
where the time goes:
time: 744 us; the launch traced here: 736 us
  waiting for transfers between devices  287 us (39%)
  matrix products  143 us (19%)
  blocking collectives  133 us (18%)
  other arithmetic  90.6 us (12%)
  local copies, waits for them, and re-layouts  45 us (6%)
  starting transfers between devices  18.5 us (2%)
  between operations  18.4 us (2%)
    reduce_scatter x1, waiting for transfers between devices, shards(): lax.psum_scatter(jnp.dot(context, w_out, preferred_element_type=jnp.float...  55.7 us
    all_to_all x4, waiting for transfers between devices, sum_at_owner(): lax.all_to_all(tiles, axis, split_axis=0, concat_axis=0, tiled=True)  51.7 us
    psum x1, blocking collectives, shards(): lax.psum((peak_full, conv_full, norm_stack), ('fsdp', 'tensor'))  40 us
    all_gather x1, blocking collectives, shards(): lax.all_gather(qkv_weight, 'fsdp', axis=1, tiled=True)  38.3 us
    reduce_scatter x1, waiting for transfers between devices, shards(): lax.psum_scatter(jnp.einsum('nf,df->nd', grad_up, w_up, preferred_element...  38 us
    reduce_scatter x1, waiting for transfers between devices, shards(): lax.psum_scatter(jnp.dot(act_low, w_down, preferred_element_type=jnp.floa...  36.1 us
    all_gather x1, waiting for transfers between devices, shards(): lax.all_gather(down_weight, 'fsdp', axis=1, tiled=True)  36 us
    all_gather x1, blocking collectives, shards(): lax.all_gather(out_weight, 'fsdp', axis=1, tiled=True)  35.1 us
  transfers between devices with their start and end apart: 14, of which 10 were waited for; matrix products, arithmetic and copies ran while one was open for 24% of the time, Pallas kernels for 0%

commit v1 on v0

--- a/solution.py
+++ b/solution.py
@@ -6,6 +6,19 @@
 HD = 64
 LANDMARKS = 64
 ITERS = 6
+
+
+def ring_gather(shard, axis, dim):
+    ways = lax.axis_size(axis)
+    up = [(d, (d + 1) % ways) for d in range(ways)]
+    down = [(d, (d - 1) % ways) for d in range(ways)]
+    earlier, later = ([shard], [shard])
+    for _ in range(ways // 2):
+        earlier.append(lax.ppermute(earlier[-1], axis, up))
+    for _ in range((ways - 1) // 2):
+        later.append(lax.ppermute(later[-1], axis, down))
+    line = jnp.concatenate([*earlier[::-1], *later[1:]], axis=dim)
+    return jnp.roll(line, (lax.axis_index(axis) - ways // 2) * shard.shape[dim], axis=dim)
 
 
 def in_blocks(value, dim, count):
@@ -110,7 +123,7 @@
         lax.all_gather(qkv_weight, "fsdp", axis=1, tiled=True),
         lax.all_gather(out_weight, "fsdp", axis=1, tiled=True),
         lax.all_gather(up_weight, "fsdp", axis=0, tiled=True),
-        lax.all_gather(down_weight, "fsdp", axis=1, tiled=True),
+        ring_gather(down_weight, "fsdp", 1),
     )
     columns = w_qkv.shape[2]
     local_heads = columns // HD

time: 744 us -> 721 us (0.969)
  waiting for transfers between devices: 287 us -> 236 us
  starting transfers between devices: 18.5 us -> 34.2 us
  local copies, waits for them, and re-layouts: 45 us -> 57.9 us
    all_gather x1 -> x0, waiting for transfers between devices: 36 us -> none  [shards(): lax.all_gather(down_weight, 'fsdp', axis=1, tiled=True)]
    all_gather x1, waiting for transfers between devices: 27.8 us -> 0.01 us  [shards(): lax.all_gather(mixed_rows.astype(jnp.bfloat16), 'tensor', axis=0, tiled=T...]
    unnamed x331 -> x356, local copies, waits for them, and re-layouts: 10.9 us -> 34.4 us
    ppermute x0 -> x7, waiting for transfers between devices: none -> 16.5 us  [the longest x4 16.5 us: ring_gather(): earlier.append(lax.ppermute(earlier[-1], axis, up))]
    ppermute x0 -> x7, starting transfers between devices: none -> 15.9 us  [the longest x3 14.3 us: ring_gather(): later.append(lax.ppermute(later[-1], axis, down))]
  transfers between devices with their start and end apart: 14 -> 20, of which waited for: 10 -> 12; matrix products, arithmetic and copies ran while one was open for 24% -> 26% of each run, Pallas kernels for 0% -> 0%
where the time goes in v1:
time: 721 us; the launch traced here: 712 us
  waiting for transfers between devices  236 us (33%)
  matrix products  139 us (19%)
  blocking collectives  134 us (19%)
  other arithmetic  92.5 us (13%)
  local copies, waits for them, and re-layouts  57.9 us (8%)
  starting transfers between devices  34.2 us (5%)
  between operations  18.5 us (3%)
    reduce_scatter x1, waiting for transfers between devices, shards(): lax.psum_scatter(jnp.dot(context, w_out, preferred_element_type=jnp.float...  55.7 us
    all_to_all x4, waiting for transfers between devices, sum_at_owner(): lax.all_to_all(tiles, axis, split_axis=0, concat_axis=0, tiled=True)  53.1 us
    psum x1, blocking collectives, shards(): lax.psum((peak_full, conv_full, norm_stack), ('fsdp', 'tensor'))  40.4 us
    all_gather x1, blocking collectives, shards(): lax.all_gather(qkv_weight, 'fsdp', axis=1, tiled=True)  38.3 us
    reduce_scatter x1, waiting for transfers between devices, shards(): lax.psum_scatter(jnp.einsum('nf,df->nd', grad_up, w_up, preferred_element...  38 us
    all_gather x1, blocking collectives, shards(): lax.all_gather(out_weight, 'fsdp', axis=1, tiled=True)  35.1 us
    unnamed x356, local copies, waits for them, and re-layouts  34.4 us
    reduce_scatter x1, waiting for transfers between devices, shards(): lax.psum_scatter(jnp.dot(act_low, w_down, preferred_element_type=jnp.floa...  34 us
  transfers between devices with their start and end apart: 20, of which 12 were waited for; matrix products, arithmetic and copies ran while one was open for 26% of the time, Pallas kernels for 0%

profile of v1, /device:TPU:0, one launch (start us, length us, event | category | flops | bytes accessed | tf_op | source)
XLA Modules:
  0.0 712.4 jit_solution(12458702161979041531)
XLA Ops:
  12.9 35.1 %all_gather.23 = bf16[192,768]{0,1:T(8,128)(2,1)} all-gather(bf16[192,96]{0,1:T(8,128)(2,1)S(1)} %copy.111), channel_id=1, replica_groups=mesh['fsdp'=8,'tensor'=4] {'fsdp'}, dimensions={1}, use_global_device_ids=true | all-gather | bytes 331776 | tf_op jit(solution)/shard_map/all_gather | solution.py:124
  48.0 38.3 %all_gather.21 = bf16[3,768,192]{2,0,1:T(4,128)(2,1)S(1)} all-gather(bf16[3,96,192]{2,0,1:T(4,128)(2,1)S(1)} %copy.100), channel_id=1, replica_groups=mesh['fsdp'=8,'tensor'=4] {'fsdp'}, dimensions={1}, use_global_device_ids=true | all-gather | bytes 995328 | tf_op jit(solution)/shard_map/all_gather | solution.py:123
  87.6 4.6 convolution_bitcast_fusion
  110.2 19.9 %pmax.7 = f32[3]{0:T(128)S(1)} all-reduce(f32[3]{0:T(128)S(1)} %reduce_max.37), channel_id=1, replica_groups=mesh['fsdp'=8,'tensor'=4] {'fsdp'}, use_global_device_ids=true, to_apply=%region_8.9 | all-reduce | flops 3 | bytes 24 | tf_op jit(solution)/shard_map/pmax | solution.py:138
  145.8 14.4 %fusion.56 = bf16[3,2048,64]{1,2,0:T(8,128)(2,1)S(1)} fusion(f32[3,64,64]{2,1,0:T(8,128)S(1)} %fusion.217, f32[3,2048,64]{1,2,0:T(8,128)S(1)} %bitcast.255, f32[3]{0:T(128)S(1)} %copy-done.131, f32[3]{0:T(128)S(1)} %copy-done.143, f32[3]{0:T(128)S(1)} %copy-done.144, f32[3]{0:T(128)S(1)} %copy-done.145, f32[3]{0:T(128)S(1)} %copy-done.146, ...), kind=kOutput, calls=%fused_computation.69 | convolution fusion | flops 328728576 | bytes 4006284 | tf_op jit(solution)/shard_map/jvp(hnj,hjd->hnd)/dot_general | solution.py:73
  164.6 55.7 %reduce-scatter.5.cloned.1.call-done = f32[512,768]{1,0:T(8,128)} async-done(((f32[2048,768]{1,0:T(8,128)}), f32[512,768]{1,0:T(8,128)}) %reduce-scatter.5.cloned.1.call-update) | async-done | bytes 1572880 | tf_op jit(solution)/shard_map/reduce_scatter | solution.py:142
  225.8 6.9 collective-permute-done
  233.4 4.7 collective-permute-start.4
  242.1 4.6 collective-permute-start.5
  250.0 5.0 collective-permute-start.6
  278.9 4.8 fusion.219
  286.4 6.7 convolution_convert_fusion.1
  293.1 34.0 %reduce-scatter.7.cloned.1.call-done = bf16[512,768]{1,0:T(8,128)(2,1)} async-done(((bf16[2048,768]{1,0:T(8,128)(2,1)}), bf16[512,768]{1,0:T(8,128)(2,1)}) %reduce-scatter.7.cloned.1.call-update) | async-done | bytes 786448 | tf_op jit(solution)/shard_map/reduce_scatter | solution.py:153
  334.2 28.4 %all-gather.12.cloned.1.call-done = bf16[2048,768]{1,0:T(8,128)(2,1)} async-done(((bf16[512,768]{1,0:T(8,128)(2,1)}), bf16[2048,768]{1,0:T(8,128)(2,1)}) %all-gather.12.cloned.1.call-update) | async-done | bytes 3145744 | tf_op jit(solution)/shard_map/all_gather | solution.py:162
  362.7 9.0 %fusion.9 = bf16[2048,768]{1,0:T(8,128)(2,1)S(1)} fusion(f32[2048,768]{1,0:T(8,128)} %copy-done.168, bf16[2048,768]{1,0:T(8,128)(2,1)} %all-gather.12.cloned.1.call-done, bf16[768,1536]{0,1:T(8,128)(2,1)} %constant_dynamic-update-slice_fusion, s32[]{:T(128)S(6)} %select_n.25), kind=kOutput, calls=%fused_computation.11 | convolution fusion | flops 2447376384 | bytes 13762564 | tf_op jit(solution)/shard_map/nd,fd->nf/dot_general | solution.py:164
  377.5 38.0 %reduce-scatter.9.cloned.1.call-done = bf16[512,768]{1,0:T(8,128)(2,1)} async-done(((bf16[2048,768]{1,0:T(8,128)(2,1)}), bf16[512,768]{1,0:T(8,128)(2,1)}) %reduce-scatter.9.cloned.1.call-update) | async-done | bytes 786448 | tf_op jit(solution)/shard_map/reduce_scatter | solution.py:167
  424.8 8.4 %convolution_convert_fusion.2 = bf16[768,768]{0,1:T(8,128)(2,1)} fusion(bf16[2048,768]{1,0:T(8,128)(2,1)} %all-gather.12.cloned.1.call-done, f32[2048,768]{1,0:T(8,128)} %copy-done.168), kind=kOutput, calls=%fused_computation.133 | convolution fusion | flops 2430664704 | bytes 10616832 | tf_op jit(solution)/shard_map/nf,nd->fd/dot_general | solution.py:163
  433.2 5.5 all-to-all-start.3
  439.4 9.9 %all-gather.14.cloned.1.call-done = bf16[2048,768]{1,0:T(8,128)(2,1)} async-done(((bf16[512,768]{1,0:T(8,128)(2,1)}), bf16[2048,768]{1,0:T(8,128)(2,1)}) %all-gather.14.cloned.1.call-update) | async-done | bytes 3145744 | tf_op jit(solution)/shard_map/all_gather | solution.py:177
  452.5 8.0 %multiply_reduce_fusion.34 = (f32[3]{0:T(128)S(1)}, f32[3]{0:T(128)S(1)}, f32[3]{0:T(128)S(1)}, f32[3]{0:T(128)S(1)}, f32[3]{0:T(128)S(1)}, /*index=5*/f32[3]{0:...) fusion(f32[3,2048,64]{1,2,0:T(8,128)S(1)} %bitcast.248, ...), kind=kLoop, calls=%fused_computation.117 | loop fusion | flops 14155722 | bytes 3145944 | tf_op jit(solution)/shard_map/transpose(jvp())/reduce_sum | solution.py:77
  476.0 7.8 %multiply_reduce_fusion.33 = (f32[3]{0:T(128)S(1)}, f32[3]{0:T(128)S(1)}, f32[3]{0:T(128)S(1)}, f32[3]{0:T(128)S(1)}, f32[3]{0:T(128)S(1)}, /*index=5*/f32[3]{0:...) fusion(f32[3,2048,64]{1,2,0:T(8,128)S(1)} %bitcast.250, ...), kind=kLoop, calls=%fused_computation.116 | loop fusion | flops 12976083 | bytes 7864536 | tf_op jit(solution)/shard_map/transpose(jvp())/reduce_sum | solution.py:77
  490.9 40.4 %all-reduce.67 = (f32[12]{0:T(128)S(1)}, f32[12,33]{1,0:T(8,128)}, f32[4,768]{1,0:T(4,128)}) all-reduce(f32[12]{0:T(128)S(1)} %fusion.173, f32[12,33]{1,0:T(8,128)S(1)} %dynamic_update_slice.7, f32[4,768]{1,0:T(4,128)} %pad_maximum_fusion.3), channel_id=1, replica_groups=mesh['fsdp'=8,'tensor'=4] {'fsdp','tensor'}, use_global_device_ids=true, to_apply=%region_26.27 | all-reduce | flops 3480 | bytes 27840 | tf_op jit(solution)/shard_map/psum | solution.py:193
  536.5 7.4 %broadcast_multiply_fusion.1 = (f32[3,2048,64]{1,2,0:T(8,128)}, f32[3,2048,64]{1,2,0:T(8,128)}, f32[3,2048,64]{1,2,0:T(8,128)}, f32[3,2048,64]{1,2,0:T(8,128)}, ...) fusion(f32[3,2048,64]{1,2,0:T(8,128)S(1)} %bitcast.251, ...), kind=kLoop, calls=%fused_computation.219 | loop fusion | flops 4718592 | bytes 20447376 | tf_op jit(solution)/shard_map/transpose(jvp())/mul | solution.py:77
  544.1 11.1 %broadcast_multiply_fusion = (f32[3,2048,64]{1,2,0:T(8,128)}, f32[3,2048,64]{1,2,0:T(8,128)}, f32[3,2048,64]{1,2,0:T(8,128)}, f32[3,2048,64]{1,2,0:T(8,128)}, f3...) fusion(f32[3,2048,64]{1,2,0:T(8,128)S(1)} %bitcast.252, ...), kind=kLoop, calls=%fused_computation.218 | loop fusion | flops 7077888 | bytes 29884632 | tf_op jit(solution)/shard_map/transpose(jvp())/mul | solution.py:77
  573.6 5.7 fusion.54
  582.2 18.5 %pad_add_fusion = f32[3,2080,64]{1,2,0:T(8,128)S(1)} fusion(f32[3,2048,64]{1,2,0:T(8,128)S(1)} %copy-done.11, f32[3,2048,64]{1,2,0:T(8,128)S(1)} %copy-done.12, f32[3,2048,64]{1,2,0:T(8,128)S(1)} %copy-done.13, f32[3,2048,64]{1,2,0:T(8,128)} %get-tuple-element.129, f32[3,2048,64]{1,2,0:T(8,128)} %get-tuple-element.130, ...), kind=kLoop, calls=%fused_computation.74 | loop fusion | flops 10383360 | bytes 44064768 | tf_op jit(solution)/shard_map/transpose(jvp())/add_any | solution.py:77
  600.8 7.5 %fusion.53 = bf16[3,2048,64]{1,2,0:T(8,128)(2,1)S(1)} fusion(f32[3,64,64]{2,1,0:T(8,128)S(1)} %copy-done.51, f32[3,2048,64]{1,2,0:T(8,128)} %get-tuple-element.119, f32[3,2048,64]{1,2,0:T(8,128)} %get-tuple-element.120, f32[3,2048,64]{1,2,0:T(8,128)} %get-tuple-element.121, f32[3,2048,64]{1,2,0:T(8,128)} %get-tuple-element.123, ...), kind=kOutput, calls=%fused_computation.66 | convolution fusion | flops 305528832 | bytes 13419264 | tf_op jit(solution)/shard_map/transpose(jvp(hin,hnd->hid))/dot_general | solution.py:71
  613.4 6.7 convolution_convert_fusion.3
  620.1 5.3 all-to-all-start.2
  628.6 25.1 %all-to-all-done.2 = bf16[8,96,768]{2,1,0:T(8,128)(2,1)} async-done(((bf16[8,96,768]{2,1,0:T(8,128)(2,1)}), bf16[8,96,768]{2,1,0:T(8,128)(2,1)}, u32[]{:S(2)}, u32[]{:S(2)}) %all-to-all-start.2) | async-done | bytes 1179680 | tf_op jit(solution)/shard_map/all_to_all | solution.py:32
  664.1 5.0 all-to-all-done.1
  678.4 23.0 %all-to-all-done = bf16[8,3,96,192]{2,3,1,0:T(8,128)(2,1)S(1)} async-done(((bf16[8,3,96,192]{2,3,1,0:T(8,128)(2,1)}), bf16[8,3,96,192]{2,3,1,0:T(8,128)(2,1)S(1)}, u32[]{:S(2)}, u32[]{:S(2)}) %all-to-all-start) | async-done | bytes 884768 | tf_op jit(solution)/shard_map/all_to_all | solution.py:32
  (559 shorter events, 188.5 us)
Async XLA Ops:
  8.0 78.3 %all-gather.6.cloned.1.call-start = ((), (), s32[]{:S(2)}) async-start(), calls=%async_computation.8 | async-start | bytes 3932160 | tf_op jit(solution)/shard_map/all_gather | solution.py:120
  10.5 209.7 %reduce-scatter.5.cloned.1.call-start = ((), (), s32[]{:S(2)}) async-start(), calls=%async_computation.9 | async-start | bytes 7864320 | tf_op jit(solution)/shard_map/reduce_scatter | solution.py:142
  145.0 15.1 %copy-start.91 = (f32[3,64,64]{2,1,0:T(8,128)}, f32[3,64,64]{2,1,0:T(8,128)S(1)}, u32[]{:S(2)}) copy-start(f32[3,64,64]{2,1,0:T(8,128)S(1)} %fusion.217) | copy-start | bytes 147460
  145.7 14.4 %copy-start.21 = (bf16[192,768]{0,1:T(8,128)(2,1)S(1)}, bf16[192,768]{0,1:T(8,128)(2,1)}, u32[]{:S(2)}) copy-start(bf16[192,768]{0,1:T(8,128)(2,1)} %all_gather.23) | copy-start | bytes 884740
  163.9 115.0 %all-gather.10.cloned.1.call-start = ((), (), s32[]{:S(2)}) async-start(), calls=%async_computation.11 | async-start | bytes 1327104 | tf_op jit(solution)/shard_map/all_gather | solution.py:125
  164.5 114.4 %all-gather.8.cloned.1.call-start = ((), (), s32[]{:S(2)}) async-start(), calls=%async_computation.10 | async-start | bytes 3932160 | tf_op jit(solution)/shard_map/all_gather | solution.py:149
  224.3 102.9 %reduce-scatter.7.cloned.1.call-start = ((), (), s32[]{:S(2)}) async-start(), calls=%async_computation.12 | async-start | bytes 3932160 | tf_op jit(solution)/shard_map/reduce_scatter | solution.py:153
  224.3 8.4 %collective-permute-start = (bf16[768,96]{0,1:T(8,128)(2,1)}, bf16[768,96]{0,1:T(8,128)(2,1)S(1)}, u32[]{:S(2)}, u32[]{:S(2)}) collective-permute-start(bf16[768,96]{0,1:T(8,128)(2,1)} %param.16), channel_id=1, source_target_pairs={{0,4},{4,8},{8,12},{12,16},{16,20},{20,24},{24,28},{28,0},{1,5},{5... | collective-permute-start | bytes 442376 | tf_op jit(solution)/shard_map/ppermute | solution.py:17
  233.4 7.9 %collective-permute-start.1 = (bf16[768,96]{0,1:T(8,128)(2,1)S(1)}, bf16[768,96]{0,1:T(8,128)(2,1)S(1)}, u32[]{:S(2)}, u32[]{:S(2)}) collective-permute-start(bf16[768,96]{0,1:T(8,128)(2,1)S(1)} %collective-permute-done), channel_id=1, source_target_pairs={{0,4},{4,8},{8,12},{12,16},{16,20},{20,24},{24,28},{28,0},{1,5},{5... | collective-permute-start | bytes 442376 | tf_op jit(solution)/shard_map/ppermute | solution.py:17
  233.4 8.8 %collective-permute-start.4 = (bf16[768,96]{0,1:T(8,128)(2,1)}, bf16[768,96]{0,1:T(8,128)(2,1)}, u32[]{:S(2)}, u32[]{:S(2)}) collective-permute-start(bf16[768,96]{0,1:T(8,128)(2,1)} %param.16), channel_id=1, source_target_pairs={{0,28},{4,0},{8,4},{12,8},{16,12},{20,16},{24,20},{28,24},{1,29},{... | collective-permute-start | bytes 442376 | tf_op jit(solution)/shard_map/ppermute | solution.py:19
  242.0 8.0 %collective-permute-start.2 = (bf16[768,96]{0,1:T(8,128)(2,1)S(1)}, bf16[768,96]{0,1:T(8,128)(2,1)}, u32[]{:S(2)}, u32[]{:S(2)}) collective-permute-start(bf16[768,96]{0,1:T(8,128)(2,1)S(1)} %collective-permute-done.1), channel_id=1, source_target_pairs={{0,4},{4,8},{8,12},{12,16},{16,20},{20,24},{24,28},{28,0},{1,5},{5... | collective-permute-start | bytes 442376 | tf_op jit(solution)/shard_map/ppermute | solution.py:17
  242.1 7.8 %collective-permute-start.5 = (bf16[768,96]{0,1:T(8,128)(2,1)}, bf16[768,96]{0,1:T(8,128)(2,1)}, u32[]{:S(2)}, u32[]{:S(2)}) collective-permute-start(bf16[768,96]{0,1:T(8,128)(2,1)} %collective-permute-done.4), channel_id=1, source_target_pairs={{0,28},{4,0},{8,4},{12,8},{16,12},{20,16},{24,20},{28,24},{1,29},{... | collective-permute-start | bytes 442376 | tf_op jit(solution)/shard_map/ppermute | solution.py:19
  250.0 8.2 %collective-permute-start.3 = (bf16[768,96]{0,1:T(8,128)(2,1)}, bf16[768,96]{0,1:T(8,128)(2,1)}, u32[]{:S(2)}, u32[]{:S(2)}) collective-permute-start(bf16[768,96]{0,1:T(8,128)(2,1)} %collective-permute-done.2), channel_id=1, source_target_pairs={{0,4},{4,8},{8,12},{12,16},{16,20},{20,24},{24,28},{28,0},{1,5},{5... | collective-permute-start | bytes 442376 | tf_op jit(solution)/shard_map/ppermute | solution.py:17
  250.0 23.1 %copy-start.83 = (bf16[768,96]{0,1:T(8,128)(2,1)S(1)}, bf16[768,96]{0,1:T(8,128)(2,1)}, u32[]{:S(2)}) copy-start(bf16[768,96]{0,1:T(8,128)(2,1)} %copy-done.82) | copy-start | bytes 442372
  250.0 23.8 %copy-start.81 = (bf16[768,96]{0,1:T(8,128)(2,1)S(1)}, bf16[768,96]{0,1:T(8,128)(2,1)}, u32[]{:S(2)}) copy-start(bf16[768,96]{0,1:T(8,128)(2,1)} %copy-done.80) | copy-start | bytes 442372
  250.0 19.3 %collective-permute-start.6 = (bf16[768,96]{0,1:T(8,128)(2,1)}, bf16[768,96]{0,1:T(8,128)(2,1)S(1)}, u32[]{:S(2)}, u32[]{:S(2)}) collective-permute-start(bf16[768,96]{0,1:T(8,128)(2,1)} %collective-permute-done.5), channel_id=1, source_target_pairs={{0,28},{4,0},{8,4},{12,8},{16,12},{20,16},{24,20},{28,24},{1,29},{... | collective-permute-start | bytes 442376 | tf_op jit(solution)/shard_map/ppermute | solution.py:19
  259.7 14.7 %copy-start.79 = (bf16[768,96]{0,1:T(8,128)(2,1)S(1)}, bf16[768,96]{0,1:T(8,128)(2,1)}, u32[]{:S(2)}) copy-start(bf16[768,96]{0,1:T(8,128)(2,1)} %param.16) | copy-start | bytes 442372
  293.1 69.6 %all-gather.12.cloned.1.call-start = ((), (), s32[]{:S(2)}) async-start(), calls=%async_computation.13 | async-start | bytes 3932160 | tf_op jit(solution)/shard_map/all_gather | solution.py:162
  334.2 81.3 %reduce-scatter.9.cloned.1.call-start = ((), (), s32[]{:S(2)}) async-start(), calls=%async_computation.14 | async-start | bytes 3932160 | tf_op jit(solution)/shard_map/reduce_scatter | solution.py:167
  377.5 71.9 %all-gather.14.cloned.1.call-start = ((), (), s32[]{:S(2)}) async-start(), calls=%async_computation.15 | async-start | bytes 3932160 | tf_op jit(solution)/shard_map/all_gather | solution.py:177
  433.2 186.9 %all-to-all-start.3 = ((bf16[8,768,96]{1,2,0:T(8,128)(2,1)}), bf16[8,768,96]{1,2,0:T(8,128)(2,1)}, u32[]{:S(2)}, u32[]{:S(2)}) async-start(bf16[8,768,96]{1,2,0:T(8,128)(2,1)} %bitcast.70), calls=%async_computation.7 | async-start | bytes 2359296 | tf_op jit(solution)/shard_map/all_to_all | solution.py:32
  438.7 263.8 %reduce-scatter.11.cloned.1.call-start = ((), (), s32[]{:S(2)}) async-start(), calls=%async_computation.16 | async-start | bytes 3932160 | tf_op jit(solution)/shard_map/reduce_scatter | solution.py:210
  484.1 47.2 %copy-start.105 = (f32[3]{0:T(128)S(1)}, f32[3]{0:T(128)}, u32[]{:S(2)}) copy-start(f32[3]{0:T(128)} %copy-done.103) | copy-start | bytes 40
  484.7 49.4 %copy-start.34 = (f32[3,64,64]{2,1,0:T(8,128)S(1)}, f32[3,64,64]{2,1,0:T(8,128)}, u32[]{:S(2)}) copy-start(f32[3,64,64]{2,1,0:T(8,128)} %copy-done.33) | copy-start | bytes 147460
  490.8 66.1 %copy-start.50 = (f32[3,64,64]{2,1,0:T(8,128)}, f32[3,64,64]{2,1,0:T(8,128)S(1)}, u32[]{:S(2)}) copy-start(f32[3,64,64]{2,1,0:T(8,128)S(1)} %fusion.221) | copy-start | bytes 147460
  582.2 18.5 %copy-start.51 = (f32[3,64,64]{2,1,0:T(8,128)S(1)}, f32[3,64,64]{2,1,0:T(8,128)}, u32[]{:S(2)}) copy-start(f32[3,64,64]{2,1,0:T(8,128)} %copy-done.50) | copy-start | bytes 147460
  613.4 12.0 %copy-start.9 = (bf16[2048,768]{1,0:T(8,128)(2,1)S(1)}, bf16[2048,768]{1,0:T(8,128)(2,1)}, u32[]{:S(2)}) copy-start(bf16[2048,768]{1,0:T(8,128)(2,1)} %all-gather.14.cloned.1.call-done) | copy-start | bytes 9437188
  620.1 33.7 %all-to-all-start.2 = ((bf16[8,96,768]{2,1,0:T(8,128)(2,1)}), bf16[8,96,768]{2,1,0:T(8,128)(2,1)}, u32[]{:S(2)}, u32[]{:S(2)}) async-start(bf16[8,96,768]{2,1,0:T(8,128)(2,1)} %bitcast.271), calls=%async_computation.6 | async-start | bytes 2359296 | tf_op jit(solution)/shard_map/all_to_all | solution.py:32
  627.3 29.9 %copy-start.78 = (bf16[3,2048,64]{1,2,0:T(8,128)(2,1)S(1)}, bf16[3,2048,64]{1,2,0:T(8,128)(2,1)}, u32[]{:S(2)}) copy-start(bf16[3,2048,64]{1,2,0:T(8,128)(2,1)} %copy-done.77) | copy-start | bytes 2359300
  653.7 15.4 %all-to-all-start.1 = ((bf16[8,192,96]{2,1,0:T(8,128)(2,1)}), bf16[8,192,96]{2,1,0:T(8,128)(2,1)S(1)}, u32[]{:S(2)}, u32[]{:S(2)}) async-start(bf16[8,192,96]{2,1,0:T(8,128)(2,1)} %bitcast.247), calls=%async_computation.5 | async-start | bytes 786432 | tf_op jit(solution)/shard_map/all_to_all | solution.py:32
  669.1 32.3 %all-to-all-start = ((bf16[8,3,96,192]{2,3,1,0:T(8,128)(2,1)}), bf16[8,3,96,192]{2,3,1,0:T(8,128)(2,1)S(1)}, u32[]{:S(2)}, u32[]{:S(2)}) async-start(bf16[8,3,96,192]{2,3,1,0:T(8,128)(2,1)} %bitcast.246), calls=%async_computation.4 | async-start | bytes 2359296 | tf_op jit(solution)/shard_map/all_to_all | solution.py:32
  677.1 25.5 %copy-start.19 = (f32[512,768]{1,0:T(8,128)S(1)}, f32[512,768]{1,0:T(8,128)}, u32[]{:S(2)}) copy-start(f32[512,768]{1,0:T(8,128)} %get-tuple-element.108) | copy-start | bytes 4718596
  (157 other events, 542.1 us)
Sparse Core Ops, SparseCore 0:
  11.0 31.2 all-gather.5
  164.1 56.1 reduce-scatter.4
  377.6 37.8 reduce-scatter.8
Sparse Core Ops, SparseCore 1:
  166.6 38.6 all-gather.9
  224.4 28.3 all-gather.7
  293.2 34.0 reduce-scatter.6
  334.3 28.3 all-gather.11
  420.9 28.3 all-gather.13
  613.5 38.8 reduce-scatter.10
